TPU v7x, 256 devices: a whole 4x4x8 slice. The times are simulated.
256 devices in a mesh: segment: 2 (over core), angle: 16 (over x_lo, z), tile: 8 (over y, x_hi).
Axes of the slice: x: 4 (x_hi: 2, x_lo: 2; x = x_hi * 2 + x_lo), y: 4, z: 8, core: 2. Of those that a mesh axis runs over, the one named last changes fastest.
Arguments:
- sinogram: float32 [64, 32, 4096], P(('segment', 'angle'), 'tile'), may hold values from -6 to 6
- paganin_width: float32 [1], replicated, may hold values from 2 to 8
- window_block: int32 [64, 8], replicated, may hold values from 0 to 28
Outputs:
- volume: float32 [8, 32, 65536], P('tile', None, ('segment', 'angle'))
All inputs are finite; a program needn't handle non-finite values.
Results may differ from a plain program's by a relative error of at most 0.0035.
Values may be sent and summed in bfloat16 or wider, within the bound.
A program may use at most 64 MiB of HBM per device.

v0:
```python
import math

import jax
import jax.numpy as jnp
from jax import lax
from jax.sharding import PartitionSpec as P

WIN = 512
BAND = 128
ROWS_DEV = 8
TCOLS = 256


def band_kernels(width):
    inner = jnp.arange(128, dtype=jnp.int32)
    offsets = (
        (jnp.arange(3, dtype=jnp.int32) - 1)[:, None, None] * 128
        + inner[None, :, None]
        - inner[None, None, :]
    )
    spread = offsets.astype(jnp.float32)
    inside = jnp.abs(offsets) <= BAND
    taps = jnp.arange(-BAND, BAND + 1).astype(jnp.float32)
    normal_total = jnp.sum(jnp.exp(-jnp.abs(taps) / width))
    paganin = jnp.where(inside, jnp.exp(-jnp.abs(spread) / width) / normal_total, 0.0)
    squared = jnp.maximum(spread * spread, 1.0)
    odd_taps = jnp.where(inside & (offsets % 2 == 1), -1.0 / (math.pi * math.pi * squared), 0.0)
    ramp = jnp.where(offsets == 0, 0.25, odd_taps)
    return (paganin, ramp)


def apply_band(rows, kernels):
    row_count, bins = rows.shape
    blocks = bins // 128
    shaped = rows.reshape(row_count, blocks, 128)
    padded = jnp.pad(shaped, ((0, 0), (1, 1), (0, 0)))
    result = jnp.zeros_like(shaped)
    for offset in range(3):
        result = result + jnp.einsum(
            "rbi,io->rbo",
            padded[:, offset : offset + blocks],
            kernels[offset],
            precision=lax.Precision.HIGHEST,
        )
    return result.reshape(row_count, bins)


def hat_block(angles, angle_total, row_first, row_count, tile_rows):
    theta = math.pi * angles.astype(jnp.float32) / angle_total
    rows_here = (row_first + jnp.arange(row_count, dtype=jnp.int32)).astype(jnp.float32) - (
        tile_rows - 1
    ) / 2.0
    columns = jnp.arange(TCOLS).astype(jnp.float32) - (TCOLS - 1) / 2.0
    across = (
        columns[None, None, :] * jnp.cos(theta)[:, None, None]
        + rows_here[None, :, None] * jnp.sin(theta)[:, None, None]
    )
    across = across.reshape(angles.shape[0], row_count * TCOLS) + WIN / 2.0
    detector = jnp.arange(WIN).astype(jnp.float32)
    weight = jnp.maximum(0.0, 1.0 - jnp.abs(across[:, None, :] - detector[None, :, None]))
    return weight.astype(jnp.bfloat16)


def accumulate_rows(total, piece, starts, row_first, angle_total, tile_rows):
    count = piece.shape[0]
    group = math.gcd(count, 4)
    turns = count // group
    blocks = piece.reshape(turns, group, piece.shape[1], piece.shape[2])
    start_groups = starts.reshape(turns, group)

    def advance(carry, item):
        block, window_starts, index = item
        angles = index * group + jnp.arange(group, dtype=jnp.int32)
        weights = hat_block(angles, angle_total, row_first, ROWS_DEV, tile_rows)
        for member in range(group):
            window = lax.dynamic_slice_in_dim(block[member], window_starts[member], WIN, 1)
            carry = carry + jnp.dot(window, weights[member], preferred_element_type=jnp.float32)
        return (carry, None)

    result, ignored = lax.scan(
        advance, total, (blocks, start_groups, jnp.arange(turns, dtype=jnp.int32))
    )
    return result


def body(sinogram, paganin_width, window_block):
    angle_local, slice_local, bins = sinogram.shape
    group_size = lax.axis_size(("segment", "angle"))
    tile_count = lax.axis_size("tile")
    angle_total = angle_local * group_size
    tile_rows = ROWS_DEV * group_size
    position = lax.axis_index(("segment", "angle"))
    tile_index = lax.axis_index("tile")
    row_first = position * ROWS_DEV
    smoothing, ramping = band_kernels(paganin_width[0])
    rows = sinogram.reshape(angle_local * slice_local, bins)
    filtered = (
        apply_band(apply_band(rows, smoothing), ramping)
        .astype(jnp.bfloat16)
        .reshape(angle_local, slice_local, bins)
    )
    slice_total = slice_local * tile_count
    empty = jnp.zeros((slice_total, ROWS_DEV * TCOLS), jnp.float32)
    own_starts = lax.dynamic_slice_in_dim(window_block, tile_index, 1, 1)[:, 0] * 128
    slab = lax.all_gather(filtered, "tile", axis=1, tiled=True)
    volume = accumulate_rows(
        empty,
        lax.all_gather(slab, ("segment", "angle"), axis=0, tiled=True),
        own_starts,
        row_first,
        angle_total,
        tile_rows,
    )
    return volume[None]


def solution(mesh):
    in_specs = (P(("segment", "angle"), "tile", None), P(), P())
    out_specs = P("tile", None, ("segment", "angle"))
    return jax.shard_map(body, mesh=mesh, in_specs=in_specs, out_specs=out_specs, check_vma=False)
```

profile of v0, /device:TPU:1, one launch (start us, length us, event | category | flops | bytes accessed | tf_op | source)
XLA Modules:
  0.0 552.2 jit_solution(8481169078443803155)
XLA Ops:
  11.6 31.7 %all_gather.6 = bf16[2,32,4096]{2,0,1:T(2,128)(2,1)S(1)} all-gather(bf16[2,4,4096]{2,0,1:T(2,128)(2,1)S(1)} %copy.6), channel_id=1, replica_groups=mesh['segment'=2,'angle'=16,'tile'=8] {'tile'}, dimensions={1}, use_global_device_ids=true | all-gather | bytes 589824 | tf_op jit(solution)/shard_map/all_gather | solution.py:105
  45.2 107.4 %all-gather.2.cloned.1.call-done = bf16[64,32,4096]{2,1,0:T(8,128)(2,1)} async-done(((bf16[2,32,4096]{2,1,0:T(8,128)(2,1)}), bf16[64,32,4096]{2,1,0:T(8,128)(2,1)}) %all-gather.2.cloned.1.call-update) | async-done | bytes 16777232 | tf_op jit(solution)/shard_map/all_gather | solution.py:108
  152.6 392.0 %while.14 = (s32[]{:T(128)}, f32[32,2048]{1,0:T(8,128)S(1)}, bf16[16,4,32,4096]{3,2,1,0:T(8,128)(2,1)}, s32[16,4]{1,0:T(8,128)S(1)}, s32[16]{0:T(128)S(1)}, /*in...) while((s32[]{:T(128)}, f32[32,2048]{1,0:T(8,128)S(1)}, ...), condition=%wide.region_2.3_spmd.clone, body=%wide.region_1.2_spmd.clone.sunk | while | flops 289753152 | bytes 19153716 | solution.py:80
  156.7 6.2 %maximum_convert_fusion.2 = bf16[4,512,2048]{2,1,0:T(8,128)(2,1)} fusion(f32[512]{0:T(512)S(1)} %iota_convert_fusion.2, f32[4,2048]{1,0:T(4,128)S(1)} %bitcast.105), kind=kLoop, calls=%fused_computation.clone.1 | loop fusion | flops 20971520 | bytes 8423424 | tf_op jit(solution)/shard_map/while/body/eval_jaxpr/convert_element_type | solution.py:61
  167.0 2.1 convolution_add_fusion.12
  174.9 2.1 convolution_add_fusion.14
  181.2 6.2 %maximum_convert_fusion.2 = bf16[4,512,2048]{2,1,0:T(8,128)(2,1)} fusion(f32[512]{0:T(512)S(1)} %iota_convert_fusion.2, f32[4,2048]{1,0:T(4,128)S(1)} %bitcast.105), kind=kLoop, calls=%fused_computation.clone.1 | loop fusion | flops 20971520 | bytes 8423424 | tf_op jit(solution)/shard_map/while/body/eval_jaxpr/convert_element_type | solution.py:61
  191.5 2.1 convolution_add_fusion.12
  195.2 2.1 convolution_add_fusion.13
  199.4 2.1 convolution_add_fusion.14
  205.7 6.2 %maximum_convert_fusion.2 = bf16[4,512,2048]{2,1,0:T(8,128)(2,1)} fusion(f32[512]{0:T(512)S(1)} %iota_convert_fusion.2, f32[4,2048]{1,0:T(4,128)S(1)} %bitcast.105), kind=kLoop, calls=%fused_computation.clone.1 | loop fusion | flops 20971520 | bytes 8423424 | tf_op jit(solution)/shard_map/while/body/eval_jaxpr/convert_element_type | solution.py:61
  219.7 2.1 convolution_add_fusion.13
  230.2 6.2 %maximum_convert_fusion.2 = bf16[4,512,2048]{2,1,0:T(8,128)(2,1)} fusion(f32[512]{0:T(512)S(1)} %iota_convert_fusion.2, f32[4,2048]{1,0:T(4,128)S(1)} %bitcast.105), kind=kLoop, calls=%fused_computation.clone.1 | loop fusion | flops 20971520 | bytes 8423424 | tf_op jit(solution)/shard_map/while/body/eval_jaxpr/convert_element_type | solution.py:61
  240.5 2.1 convolution_add_fusion.12
  244.3 2.1 convolution_add_fusion.13
  254.7 6.2 %maximum_convert_fusion.2 = bf16[4,512,2048]{2,1,0:T(8,128)(2,1)} fusion(f32[512]{0:T(512)S(1)} %iota_convert_fusion.2, f32[4,2048]{1,0:T(4,128)S(1)} %bitcast.105), kind=kLoop, calls=%fused_computation.clone.1 | loop fusion | flops 20971520 | bytes 8423424 | tf_op jit(solution)/shard_map/while/body/eval_jaxpr/convert_element_type | solution.py:61
  265.0 2.1 convolution_add_fusion.12
  272.9 2.1 convolution_add_fusion.14
  279.2 6.2 %maximum_convert_fusion.2 = bf16[4,512,2048]{2,1,0:T(8,128)(2,1)} fusion(f32[512]{0:T(512)S(1)} %iota_convert_fusion.2, f32[4,2048]{1,0:T(4,128)S(1)} %bitcast.105), kind=kLoop, calls=%fused_computation.clone.1 | loop fusion | flops 20971520 | bytes 8423424 | tf_op jit(solution)/shard_map/while/body/eval_jaxpr/convert_element_type | solution.py:61
  289.5 2.1 convolution_add_fusion.12
  293.3 2.1 convolution_add_fusion.13
  297.4 2.1 convolution_add_fusion.14
  303.7 6.2 %maximum_convert_fusion.2 = bf16[4,512,2048]{2,1,0:T(8,128)(2,1)} fusion(f32[512]{0:T(512)S(1)} %iota_convert_fusion.2, f32[4,2048]{1,0:T(4,128)S(1)} %bitcast.105), kind=kLoop, calls=%fused_computation.clone.1 | loop fusion | flops 20971520 | bytes 8423424 | tf_op jit(solution)/shard_map/while/body/eval_jaxpr/convert_element_type | solution.py:61
  317.8 2.1 convolution_add_fusion.13
  328.2 6.2 %maximum_convert_fusion.2 = bf16[4,512,2048]{2,1,0:T(8,128)(2,1)} fusion(f32[512]{0:T(512)S(1)} %iota_convert_fusion.2, f32[4,2048]{1,0:T(4,128)S(1)} %bitcast.105), kind=kLoop, calls=%fused_computation.clone.1 | loop fusion | flops 20971520 | bytes 8423424 | tf_op jit(solution)/shard_map/while/body/eval_jaxpr/convert_element_type | solution.py:61
  342.3 2.1 convolution_add_fusion.13
  352.7 6.2 %maximum_convert_fusion.2 = bf16[4,512,2048]{2,1,0:T(8,128)(2,1)} fusion(f32[512]{0:T(512)S(1)} %iota_convert_fusion.2, f32[4,2048]{1,0:T(4,128)S(1)} %bitcast.105), kind=kLoop, calls=%fused_computation.clone.1 | loop fusion | flops 20971520 | bytes 8423424 | tf_op jit(solution)/shard_map/while/body/eval_jaxpr/convert_element_type | solution.py:61
  363.0 2.1 convolution_add_fusion.12
  370.9 2.1 convolution_add_fusion.14
  377.2 6.2 %maximum_convert_fusion.2 = bf16[4,512,2048]{2,1,0:T(8,128)(2,1)} fusion(f32[512]{0:T(512)S(1)} %iota_convert_fusion.2, f32[4,2048]{1,0:T(4,128)S(1)} %bitcast.105), kind=kLoop, calls=%fused_computation.clone.1 | loop fusion | flops 20971520 | bytes 8423424 | tf_op jit(solution)/shard_map/while/body/eval_jaxpr/convert_element_type | solution.py:61
  387.5 2.1 convolution_add_fusion.12
  391.3 2.1 convolution_add_fusion.13
  395.4 2.1 convolution_add_fusion.14
  401.8 6.2 %maximum_convert_fusion.2 = bf16[4,512,2048]{2,1,0:T(8,128)(2,1)} fusion(f32[512]{0:T(512)S(1)} %iota_convert_fusion.2, f32[4,2048]{1,0:T(4,128)S(1)} %bitcast.105), kind=kLoop, calls=%fused_computation.clone.1 | loop fusion | flops 20971520 | bytes 8423424 | tf_op jit(solution)/shard_map/while/body/eval_jaxpr/convert_element_type | solution.py:61
  415.8 2.1 convolution_add_fusion.13
  426.3 6.2 %maximum_convert_fusion.2 = bf16[4,512,2048]{2,1,0:T(8,128)(2,1)} fusion(f32[512]{0:T(512)S(1)} %iota_convert_fusion.2, f32[4,2048]{1,0:T(4,128)S(1)} %bitcast.105), kind=kLoop, calls=%fused_computation.clone.1 | loop fusion | flops 20971520 | bytes 8423424 | tf_op jit(solution)/shard_map/while/body/eval_jaxpr/convert_element_type | solution.py:61
  440.3 2.1 convolution_add_fusion.13
  450.8 6.2 %maximum_convert_fusion.2 = bf16[4,512,2048]{2,1,0:T(8,128)(2,1)} fusion(f32[512]{0:T(512)S(1)} %iota_convert_fusion.2, f32[4,2048]{1,0:T(4,128)S(1)} %bitcast.105), kind=kLoop, calls=%fused_computation.clone.1 | loop fusion | flops 20971520 | bytes 8423424 | tf_op jit(solution)/shard_map/while/body/eval_jaxpr/convert_element_type | solution.py:61
  461.0 2.1 convolution_add_fusion.12
  469.0 2.1 convolution_add_fusion.14
  475.3 6.2 %maximum_convert_fusion.2 = bf16[4,512,2048]{2,1,0:T(8,128)(2,1)} fusion(f32[512]{0:T(512)S(1)} %iota_convert_fusion.2, f32[4,2048]{1,0:T(4,128)S(1)} %bitcast.105), kind=kLoop, calls=%fused_computation.clone.1 | loop fusion | flops 20971520 | bytes 8423424 | tf_op jit(solution)/shard_map/while/body/eval_jaxpr/convert_element_type | solution.py:61
  485.5 2.1 convolution_add_fusion.12
  489.3 2.1 convolution_add_fusion.13
  493.5 2.1 convolution_add_fusion.14
  499.8 6.2 %maximum_convert_fusion.2 = bf16[4,512,2048]{2,1,0:T(8,128)(2,1)} fusion(f32[512]{0:T(512)S(1)} %iota_convert_fusion.2, f32[4,2048]{1,0:T(4,128)S(1)} %bitcast.105), kind=kLoop, calls=%fused_computation.clone.1 | loop fusion | flops 20971520 | bytes 8423424 | tf_op jit(solution)/shard_map/while/body/eval_jaxpr/convert_element_type | solution.py:61
  513.8 2.1 convolution_add_fusion.13
  524.3 6.2 %maximum_convert_fusion.2 = bf16[4,512,2048]{2,1,0:T(8,128)(2,1)} fusion(f32[512]{0:T(512)S(1)} %iota_convert_fusion.2, f32[4,2048]{1,0:T(4,128)S(1)} %bitcast.105), kind=kLoop, calls=%fused_computation.clone.1 | loop fusion | flops 20971520 | bytes 8423424 | tf_op jit(solution)/shard_map/while/body/eval_jaxpr/convert_element_type | solution.py:61
  538.3 2.1 convolution_add_fusion.13
  (233 shorter events, 106.8 us)
Async XLA Ops:
  6.5 146.0 %all-gather.2.cloned.1.call-start = ((), (), s32[]{:S(2)}) async-start(), calls=%async_computation | async-start | bytes 17301504 | tf_op jit(solution)/shard_map/all_gather | solution.py:108
  544.6 0.7 copy-start
Sparse Core Ops, SparseCore 0:
  44.5 108.0 all-gather.1
where the time goes:
time: 556 us; the launch traced here: 552 us
  matrix products  138 us (25%)
  loops' own time  131 us (24%)
  waiting for transfers between devices  107 us (19%)
  other arithmetic  106 us (19%)
  blocking collectives  31.7 us (6%)
  local copies, waits for them, and re-layouts  23.8 us (4%)
  between operations  14.1 us (3%)
    dot_general x64, matrix products, advance(): jnp.dot(window, weights[member], preferred_element_type=jnp.float32)  137 us
    another operation x1, loops' own time, accumulate_rows(): lax.scan(advance, total, (blocks, start_groups, jnp.arange(turns, dtype=j...  131 us
    all_gather x1, waiting for transfers between devices, body(): lax.all_gather(slab, ('segment', 'angle'), axis=0, tiled=True)  107 us
    convert_element_type x16, other arithmetic, hat_block(): return weight.astype(jnp.bfloat16)  99 us
    all_gather x1, blocking collectives, body(): slab = lax.all_gather(filtered, 'tile', axis=1, tiled=True)  31.7 us
  transfers between devices with their start and end apart: 1, of which 1 were waited for; matrix products, arithmetic and copies ran while one was open for 0% of the time, Pallas kernels for 0%

commit v1 on v0

v1 whole, which is shorter than its diff:
```python
import functools
import math

import jax
import jax.numpy as jnp
import numpy as np
from jax import lax
from jax.experimental import pallas as pl
from jax.experimental.pallas import tpu as pltpu
from jax.sharding import PartitionSpec as P

MESH = pl.DeviceIdType.MESH
LANES = 128
BAND = 128
ROWS_DEV = 8
TCOLS = 256
ANGLES = 64
TROWS = 256
TILES = 8
ZS = 8
XS = 2
BLOCKS = 32
KEEP = 3
BINS_SHIFT = 64
CENTRE = 256 - BINS_SHIFT

F32 = jnp.float32
BF16 = jnp.bfloat16

GATHER = lax.GatherDimensionNumbers(
    offset_dims=(),
    collapsed_slice_dims=(1,),
    start_index_map=(1,),
    operand_batching_dims=(0,),
    start_indices_batching_dims=(0,),
)


def lane_gather(values, index):
    return lax.gather(
        values, index[:, :, None], GATHER, (1, 1), mode=lax.GatherScatterMode.PROMISE_IN_BOUNDS
    )


def iota(shape, axis):
    return lax.broadcasted_iota(jnp.int32, shape, axis)


def split(value):
    high = value.astype(BF16)
    return high, (value - high.astype(F32)).astype(BF16)


def dot3(left, right):
    left_high, left_low = split(left)
    right_high, right_low = split(right)
    return (
        jnp.dot(left_high, right_high, preferred_element_type=F32)
        + jnp.dot(left_low, right_high, preferred_element_type=F32)
        + jnp.dot(left_high, right_low, preferred_element_type=F32)
    )


def smoothing_band(width):
    shape = (3 * LANES, LANES)
    offset = iota(shape, 0) - LANES - iota(shape, 1)
    spread = jnp.abs(offset).astype(F32)
    taps = jnp.exp(-(iota((1, LANES), 1) + 1).astype(F32) / width)
    total = 1.0 + 2.0 * jnp.sum(taps)
    return jnp.where(jnp.abs(offset) <= BAND, jnp.exp(-spread / width) / total, 0.0)


def ramp_band():
    shape = (4 * LANES, LANES)
    offset = iota(shape, 0) - LANES - BINS_SHIFT - iota(shape, 1)
    size = jnp.abs(offset)
    spread = size.astype(F32)
    odd = jnp.where(
        (size <= BAND) & (size % 2 == 1),
        -1.0 / (math.pi * math.pi * jnp.maximum(spread * spread, 1.0)),
        0.0,
    )
    return jnp.where(offset == 0, 0.25, odd)


def filter_rows(sino_ref, width_ref, padded, smooth, filtered):
    zero = jnp.zeros((8, LANES), F32)
    padded[0:8] = zero
    padded[264:272] = zero
    smooth[0:8] = zero
    smooth[264:272] = zero
    for block in range(BLOCKS):
        columns = slice(block * LANES, (block + 1) * LANES)
        padded[(block + 1) * 8 : (block + 2) * 8] = jnp.concatenate(
            [sino_ref[0, :, columns], sino_ref[1, :, columns]], axis=0
        )
    left = jnp.concatenate([padded[8 * k : 8 * k + 256] for k in range(3)], axis=1)
    width = jnp.full((1, 1), width_ref[0], F32)
    smooth[8:264] = dot3(left, smoothing_band(width))
    left = jnp.concatenate([smooth[8 * k : 8 * k + 248] for k in range(4)], axis=1)
    filtered[...] = dot3(left, ramp_band()).reshape(BLOCKS - 1, 8, LANES)


def kernel(
    sino_ref,
    width_ref,
    window_ref,
    cos_ref,
    sin_ref,
    out_ref,
    padded,
    smooth,
    filtered,
    outgoing,
    held,
    total,
    partner_part,
    arrived_part,
    plane_send,
    plane_recv,
    ring_send,
    ring_recv,
    local_sem,
    part_send,
    part_recv,
):
    core = lax.axis_index("segment")
    chip = lax.axis_index("angle")
    tile = lax.axis_index("tile")
    x_low = chip // ZS
    z = chip % ZS
    spot = x_low * TILES + tile
    up = (z + 1) % ZS
    down = (z + ZS - 1) % ZS

    def plane_device(step):
        other = (spot + step) % (XS * TILES)
        return (core, (other // TILES) * ZS + z, other % TILES)

    neighbours = {0: (core, x_low * ZS + up, tile), 1: (core, x_low * ZS + down, tile)}
    partner = (1 - core, chip, tile)

    barrier = pltpu.get_barrier_semaphore()
    for step in range(1, XS * TILES):
        pl.semaphore_signal(barrier, inc=1, device_id=plane_device(step), device_id_type=MESH)
    for way in (0, 1):
        pl.semaphore_signal(barrier, inc=1, device_id=neighbours[way], device_id_type=MESH)
    pl.semaphore_signal(barrier, inc=1, device_id=partner, device_id_type=MESH)

    filter_rows(sino_ref, width_ref, padded, smooth, filtered)

    lower = iota((8, LANES), 0) < 4
    first_angle = (core * XS * ZS + chip) * 2
    for other in range(TILES):
        first = window_ref[first_angle, other]
        second = window_ref[first_angle + 1, other]
        for block in range(KEEP):
            outgoing[other, block] = jnp.where(
                lower, filtered[first + block], filtered[second + block]
            ).astype(BF16)

    @pl.loop(0, 32)
    def _(unit):
        total[unit] = jnp.zeros((64, LANES), F32)

    pl.semaphore_wait(barrier, XS * TILES + 2)

    own = pltpu.make_async_copy(outgoing.at[tile], held.at[z, x_low, tile], local_sem)
    own.start()
    sends = []
    for step in range(1, XS * TILES):
        copy = pltpu.make_async_remote_copy(
            src_ref=outgoing.at[(spot + step) % TILES],
            dst_ref=held.at[z, x_low, tile],
            send_sem=plane_send.at[step],
            recv_sem=plane_recv.at[step],
            device_id=plane_device(step),
            device_id_type=MESH,
        )
        copy.start()
        sends.append(copy)

    def ring_copy(way, hop, part):
        source = (z + ZS - hop) % ZS if way == 0 else (z + hop) % ZS
        return pltpu.make_async_remote_copy(
            src_ref=held.at[source, part],
            dst_ref=held.at[source, part],
            send_sem=ring_send.at[way, hop, part],
            recv_sem=ring_recv.at[way, hop, part],
            device_id=neighbours[way],
            device_id_type=MESH,
        )

    lane = iota((8, LANES), 1)
    lane_f = lane.astype(F32)
    lane16 = iota((16, LANES), 1).astype(jnp.int16)
    last_lane = lane == LANES - 1
    own_row = ((core * XS * ZS + chip) * ROWS_DEV).astype(F32) - (TROWS - 1) / 2.0
    partner_row = (((1 - core) * XS * ZS + chip) * ROWS_DEV).astype(F32) - (TROWS - 1) / 2.0

    def compute(source, part):
        angle = (core * XS * ZS + part * ZS + source) * 2
        cosine = jnp.where(lower, cos_ref[angle], cos_ref[angle + 1])
        sine = jnp.where(lower, sin_ref[angle], sin_ref[angle + 1])
        values, slopes = [], []
        for pair in range(TILES // 2):
            value_row, slope_row = [], []
            here = [
                [held[source, part, 2 * pair + half, block].astype(F32) for block in range(KEEP)]
                for half in (0, 1)
            ]
            moved = [[pltpu.roll(v, LANES - 1, 1) for v in row] for row in here]
            for block in range(KEEP):
                diffs = []
                for half in (0, 1):
                    after = moved[half][min(block + 1, KEEP - 1)]
                    diffs.append(
                        jnp.where(last_lane, after, moved[half][block]) - here[half][block]
                    )
                value_row.append(
                    jnp.concatenate([here[0][block], here[1][block]], axis=0).astype(BF16)
                )
                slope_row.append(jnp.concatenate(diffs, axis=0).astype(BF16))
            values.append(value_row)
            slopes.append(slope_row)
        spans, starts = [], []
        for half in (0, 1):
            left_end = half * LANES - (TCOLS - 1) / 2.0
            spans.append((lane_f + left_end) * cosine + float(CENTRE))
            end = jnp.where(cosine >= 0.0, left_end, left_end + LANES - 1.0)
            starts.append(end * cosine + float(CENTRE))
        for row in range(2 * ROWS_DEV):
            y = (partner_row if row < ROWS_DEV else own_row) + float(row % ROWS_DEV)
            lift = sine * y
            for half in (0, 1):
                unit = row * 2 + half
                u = spans[half] + lift
                k = u.astype(jnp.int32)
                part_way = u - k.astype(F32)
                k = k & (LANES - 1)
                index = jnp.concatenate([k, k], axis=0).astype(jnp.int16)
                begin = (starts[half] + lift).astype(jnp.int32)
                begin = jnp.concatenate([begin, begin], axis=0).astype(jnp.int16)
                past0 = begin > lane16
                past1 = begin > lane16 + jnp.int16(LANES)
                for pair in range(TILES // 2):
                    v = values[pair]
                    d = slopes[pair]
                    v = jnp.where(past1, v[2], jnp.where(past0, v[1], v[0]))
                    d = jnp.where(past1, d[2], jnp.where(past0, d[1], d[0]))
                    v = lane_gather(v, index).astype(F32)
                    d = lane_gather(d, index).astype(F32)
                    for half_row in (0, 1):
                        rows = slice(half_row * 8, half_row * 8 + 8)
                        at = slice(pair * 16 + half_row * 8, pair * 16 + half_row * 8 + 8)
                        total[unit, at] += v[rows] + part_way * d[rows]

    own.wait()
    for step in range(1, XS * TILES):
        sends[step - 1].wait_recv()
    for part in range(XS):
        for way in (0, 1):
            ring_copy(way, 0, part).start()

    @pl.loop(0, XS)
    def _(part):
        compute(z, part)

    @pl.loop(1, 4)
    def _(hop):
        @pl.loop(0, XS)
        def _(part):
            for way in (0, 1):
                ring_copy(way, hop - 1, part).wait_recv()

                @pl.when((hop < 3) | (part == way))
                def _():
                    ring_copy(way, hop, part).start()

            @pl.loop(0, 2)
            def _(way):
                compute(jnp.where(way == 0, (z + ZS - hop) % ZS, (z + hop) % ZS), part)

    ring_copy(0, 3, 0).wait_recv()
    ring_copy(1, 3, 1).wait_recv()

    @pl.loop(0, XS)
    def _(part):
        compute((z + 4) % ZS, part)

    def fold(unit):
        result = []
        for group in range(4):
            pieces = []
            for half in (0, 1):
                v = total[unit, group * 16 + half * 8 : group * 16 + half * 8 + 8]
                pieces.append(v + pltpu.roll(v, 4, 0))
            result.append(jnp.where(lower, pieces[0], pieces[1]))
        return jnp.concatenate(result, axis=0)

    for unit in range(16):
        partner_part[unit] = fold(unit)
    swaps = []
    swap = pltpu.make_async_remote_copy(
        src_ref=partner_part,
        dst_ref=arrived_part,
        send_sem=part_send,
        recv_sem=part_recv,
        device_id=partner,
        device_id_type=MESH,
    )
    swap.start()
    for unit in range(16):
        out_ref[0, :, unit * LANES : (unit + 1) * LANES] = fold(unit + 16)
    swap.wait_recv()
    for unit in range(16):
        out_ref[0, :, unit * LANES : (unit + 1) * LANES] += arrived_part[unit]

    swap.wait_send()
    for copy in sends:
        copy.wait_send()
    for hop in range(4):
        for part in range(XS):
            for way in (0, 1):
                if hop < 3 or part == way:
                    ring_copy(way, hop, part).wait_send()


def body(sinogram, paganin_width, window_block):
    angles = np.pi * np.arange(ANGLES) / ANGLES
    cosines = jnp.asarray(np.cos(angles).astype(np.float32))
    sines = jnp.asarray(np.sin(angles).astype(np.float32))
    smem = pl.BlockSpec(memory_space=pltpu.SMEM)
    vmem = pl.BlockSpec(memory_space=pltpu.VMEM)
    return pl.pallas_call(
        kernel,
        out_shape=jax.ShapeDtypeStruct((1, 32, ROWS_DEV * TCOLS), F32),
        in_specs=[vmem, smem, smem, smem, smem],
        out_specs=vmem,
        scratch_shapes=[
            pltpu.VMEM((272, LANES), F32),
            pltpu.VMEM((272, LANES), F32),
            pltpu.VMEM((BLOCKS - 1, 8, LANES), F32),
            pltpu.VMEM((TILES, KEEP, 8, LANES), BF16),
            pltpu.VMEM((ZS, XS, TILES, KEEP, 8, LANES), BF16),
            pltpu.VMEM((32, 64, LANES), F32),
            pltpu.VMEM((16, 32, LANES), F32),
            pltpu.VMEM((16, 32, LANES), F32),
            pltpu.SemaphoreType.DMA((XS * TILES,)),
            pltpu.SemaphoreType.DMA((XS * TILES,)),
            pltpu.SemaphoreType.DMA((2, 4, XS)),
            pltpu.SemaphoreType.DMA((2, 4, XS)),
            pltpu.SemaphoreType.DMA,
            pltpu.SemaphoreType.DMA,
            pltpu.SemaphoreType.DMA,
        ],
        compiler_params=pltpu.CompilerParams(collective_id=0, has_side_effects=True),
    )(sinogram, paganin_width, window_block, cosines, sines)


def solution(mesh):
    in_specs = (P(("segment", "angle"), "tile", None), P(), P())
    out_specs = P("tile", None, ("segment", "angle"))
    return jax.shard_map(body, mesh=mesh, in_specs=in_specs, out_specs=out_specs, check_vma=False)
```

time: 556 us -> 38.8 us (0.07)
  matrix products: 138 us -> 0 us
  loops' own time: 131 us -> 0 us
  waiting for transfers between devices: 107 us -> 0 us
  other arithmetic: 106 us -> 0 us
  Pallas kernels: 0 us -> 34.9 us
  blocking collectives: 31.7 us -> 0 us
  local copies, waits for them, and re-layouts: 23.8 us -> 3.06 us
  between operations: 14.1 us -> 0.66 us
    dot_general x70 -> x0, matrix products: 138 us -> none  [the longest x64 137 us: advance(): jnp.dot(window, weights[member], preferred_element_type=jnp.float32)]
    another operation x1 -> x0, loops' own time: 131 us -> none  [accumulate_rows(): lax.scan(advance, total, (blocks, start_groups, jnp.arange(turns, dtype=j...]
    all_gather x1 -> x0, waiting for transfers between devices: 107 us -> none  [body(): lax.all_gather(slab, ('segment', 'angle'), axis=0, tiled=True)]
    convert_element_type x32 -> x0, other arithmetic: 99.1 us -> none  [the longest x16 99 us: hat_block(): return weight.astype(jnp.bfloat16)]
    pallas_call x0 -> x1, Pallas kernels: none -> 34.9 us  [body(): pl.pallas_call(kernel, out_shape=jax.ShapeDtypeStruct((1, 32, ROWS_DEV *...]
    all_gather x1 -> x0, blocking collectives: 31.7 us -> none  [body(): slab = lax.all_gather(filtered, 'tile', axis=1, tiled=True)]
    slice x16 -> x0, local copies, waits for them, and re-layouts: 10.5 us -> none  [advance(): window_starts[member]]
    dynamic_slice x32 -> x0, local copies, waits for them, and re-layouts: 10 us -> none  [accumulate_rows(): lax.scan(advance, total, (blocks, start_groups, jnp.arange(turns, dtype=j...]
  transfers between devices with their start and end apart: 1 -> 0, of which waited for: 1 -> 0; matrix products, arithmetic and copies ran while one was open for 0% -> 0% of each run, Pallas kernels for 0% -> 0%
where the time goes in v1:
time: 38.8 us; the launch traced here: 38.6 us
  Pallas kernels  34.9 us (90%)
  local copies, waits for them, and re-layouts  3.06 us (8%)
  between operations  0.66 us (2%)
    pallas_call x1, Pallas kernels, body(): pl.pallas_call(kernel, out_shape=jax.ShapeDtypeStruct((1, 32, ROWS_DEV *...  34.9 us
    unnamed x2, local copies, waits for them, and re-layouts  3.06 us

profile of v1, /device:TPU:1, one launch (start us, length us, event | category | flops | bytes accessed | tf_op | source)
XLA Modules:
  0.0 38.6 jit_solution(2673296855230032993)
XLA Ops:
  0.7 1.4 %copy.6.window_ref = s32[64,8]{1,0:T(8,128)} copy(s32[64,8]{0,1:T(8,128)} %param.7) | data formatting | bytes 4096 | tf_op args[2]
  2.0 34.9 %shard_map.55 = f32[1,32,2048]{2,1,0:T(8,128)} custom-call(f32[2,4,4096]{2,1,0:T(4,128)} %sino_ref.1, f32[1]{0:T(128)S(6)} %copy.8.width_ref, s32[64,8]{1,0:T(8,128)} %copy.6.window_ref, f32[64]{0:T(128)} %constant.4.clone.cos_ref, f32[64]{0:T(128)} %constant.5.clone.sin_ref), custom_call_target="tpu_custom_call" | custom-call | tf_op jit(solution)/shard_map/pallas_call | solution.py:335
  36.9 1.7 %copy.9 = f32[1,32,2048]{2,1,0:T(8,128)} copy(f32[1,32,2048]{2,1,0:T(8,128)} %shard_map.55) | data formatting | bytes 524288

commit v2 on v1

--- a/solution.py
+++ b/solution.py
@@ -23,6 +23,16 @@
 KEEP = 3
 BINS_SHIFT = 64
 CENTRE = 256 - BINS_SHIFT
+LAG = 3
+
+
+def ring_distance(step):
+    return sum(min(part, 4 - part) for part in step)
+
+
+PLANE_STEPS = sorted(
+    ((a, b) for a in range(4) for b in range(4) if a or b), key=ring_distance, reverse=True
+)
 
 F32 = jnp.float32
 BF16 = jnp.bfloat16
@@ -111,15 +121,15 @@
     padded,
     smooth,
     filtered,
-    outgoing,
+    column,
     held,
     total,
     partner_part,
     arrived_part,
+    column_send,
+    column_recv,
     plane_send,
     plane_recv,
-    ring_send,
-    ring_recv,
     local_sem,
     part_send,
     part_recv,
@@ -127,24 +137,27 @@
     core = lax.axis_index("segment")
     chip = lax.axis_index("angle")
     tile = lax.axis_index("tile")
-    x_low = chip // ZS
     z = chip % ZS
-    spot = x_low * TILES + tile
-    up = (z + 1) % ZS
-    down = (z + ZS - 1) % ZS
-
-    def plane_device(step):
-        other = (spot + step) % (XS * TILES)
-        return (core, (other // TILES) * ZS + z, other % TILES)
-
-    neighbours = {0: (core, x_low * ZS + up, tile), 1: (core, x_low * ZS + down, tile)}
+    spot = (chip // ZS) * TILES + tile
+    x = (tile % 2) * 2 + chip // ZS
+    y = tile // 2
+
+    def plane_peer(step):
+        other_x = (x + step[0]) % 4
+        other_y = (y + step[1]) % 4
+        other_tile = other_y * 2 + other_x // 2
+        return other_tile, (core, (other_x % 2) * ZS + z, other_tile)
+
+    def column_peer(shift):
+        return (core, chip - z + (z + shift) % ZS, tile)
+
     partner = (1 - core, chip, tile)
 
     barrier = pltpu.get_barrier_semaphore()
-    for step in range(1, XS * TILES):
-        pl.semaphore_signal(barrier, inc=1, device_id=plane_device(step), device_id_type=MESH)
-    for way in (0, 1):
-        pl.semaphore_signal(barrier, inc=1, device_id=neighbours[way], device_id_type=MESH)
+    for step in PLANE_STEPS:
+        pl.semaphore_signal(barrier, inc=1, device_id=plane_peer(step)[1], device_id_type=MESH)
+    for shift in range(1, ZS):
+        pl.semaphore_signal(barrier, inc=1, device_id=column_peer(shift), device_id_type=MESH)
     pl.semaphore_signal(barrier, inc=1, device_id=partner, device_id_type=MESH)
 
     filter_rows(sino_ref, width_ref, padded, smooth, filtered)
@@ -152,10 +165,10 @@
     lower = iota((8, LANES), 0) < 4
     first_angle = (core * XS * ZS + chip) * 2
     for other in range(TILES):
-        first = window_ref[first_angle, other]
-        second = window_ref[first_angle + 1, other]
+        first = window_ref[other, first_angle]
+        second = window_ref[other, first_angle + 1]
         for block in range(KEEP):
-            outgoing[other, block] = jnp.where(
+            column[z, other, block] = jnp.where(
                 lower, filtered[first + block], filtered[second + block]
             ).astype(BF16)
 
@@ -163,33 +176,50 @@
     def _(unit):
         total[unit] = jnp.zeros((64, LANES), F32)
 
-    pl.semaphore_wait(barrier, XS * TILES + 2)
-
-    own = pltpu.make_async_copy(outgoing.at[tile], held.at[z, x_low, tile], local_sem)
-    own.start()
-    sends = []
-    for step in range(1, XS * TILES):
-        copy = pltpu.make_async_remote_copy(
-            src_ref=outgoing.at[(spot + step) % TILES],
-            dst_ref=held.at[z, x_low, tile],
-            send_sem=plane_send.at[step],
-            recv_sem=plane_recv.at[step],
-            device_id=plane_device(step),
+    pl.semaphore_wait(barrier, len(PLANE_STEPS) + ZS)
+
+    def column_shift(turn):
+        far = (ZS + 1 - turn) // 2
+        return jnp.where(turn == 0, 0, jnp.where(turn % 2 == 0, far, ZS - far))
+
+    def column_copy(turn):
+        return pltpu.make_async_remote_copy(
+            src_ref=column.at[z],
+            dst_ref=column.at[z],
+            send_sem=column_send.at[turn],
+            recv_sem=column_recv.at[turn],
+            device_id=column_peer(column_shift(turn)),
             device_id_type=MESH,
         )
-        copy.start()
-        sends.append(copy)
-
-    def ring_copy(way, hop, part):
-        source = (z + ZS - hop) % ZS if way == 0 else (z + hop) % ZS
-        return pltpu.make_async_remote_copy(
-            src_ref=held.at[source, part],
-            dst_ref=held.at[source, part],
-            send_sem=ring_send.at[way, hop, part],
-            recv_sem=ring_recv.at[way, hop, part],
-            device_id=neighbours[way],
-            device_id_type=MESH,
+
+    for turn in range(1, ZS):
+        column_copy(turn).start()
+
+    def slot(turn):
+        return (z + ZS - column_shift(turn)) % ZS
+
+    def own_copy(turn):
+        return pltpu.make_async_copy(
+            column.at[slot(turn), tile], held.at[slot(turn), spot], local_sem.at[turn]
         )
+
+    def spread(turn):
+        source = slot(turn)
+        own_copy(turn).start()
+        for step in PLANE_STEPS:
+            other_tile, device = plane_peer(step)
+            pltpu.make_async_remote_copy(
+                src_ref=column.at[source, other_tile],
+                dst_ref=held.at[source, spot],
+                send_sem=plane_send.at[turn],
+                recv_sem=plane_recv.at[turn],
+                device_id=device,
+                device_id_type=MESH,
+            ).start()
+
+    def all_of_plane(turn, sem):
+        some = held.at[slot(turn), pl.ds(0, len(PLANE_STEPS))]
+        return pltpu.make_async_copy(some, some, sem.at[turn])
 
     lane = iota((8, LANES), 1)
     lane_f = lane.astype(F32)
@@ -200,13 +230,14 @@
 
     def compute(source, part):
         angle = (core * XS * ZS + part * ZS + source) * 2
+        spots = part * TILES
         cosine = jnp.where(lower, cos_ref[angle], cos_ref[angle + 1])
         sine = jnp.where(lower, sin_ref[angle], sin_ref[angle + 1])
         values, slopes = [], []
         for pair in range(TILES // 2):
             value_row, slope_row = [], []
             here = [
-                [held[source, part, 2 * pair + half, block].astype(F32) for block in range(KEEP)]
+                [held[source, spots + 2 * pair + half, block].astype(F32) for block in range(KEEP)]
                 for half in (0, 1)
             ]
             moved = [[pltpu.roll(v, LANES - 1, 1) for v in row] for row in here]
@@ -255,38 +286,25 @@
                         at = slice(pair * 16 + half_row * 8, pair * 16 + half_row * 8 + 8)
                         total[unit, at] += v[rows] + part_way * d[rows]
 
-    own.wait()
-    for step in range(1, XS * TILES):
-        sends[step - 1].wait_recv()
-    for part in range(XS):
-        for way in (0, 1):
-            ring_copy(way, 0, part).start()
-
-    @pl.loop(0, XS)
-    def _(part):
-        compute(z, part)
-
-    @pl.loop(1, 4)
-    def _(hop):
-        @pl.loop(0, XS)
-        def _(part):
-            for way in (0, 1):
-                ring_copy(way, hop - 1, part).wait_recv()
-
-                @pl.when((hop < 3) | (part == way))
-                def _():
-                    ring_copy(way, hop, part).start()
-
-            @pl.loop(0, 2)
-            def _(way):
-                compute(jnp.where(way == 0, (z + ZS - hop) % ZS, (z + hop) % ZS), part)
-
-    ring_copy(0, 3, 0).wait_recv()
-    ring_copy(1, 3, 1).wait_recv()
-
-    @pl.loop(0, XS)
-    def _(part):
-        compute((z + 4) % ZS, part)
+    @pl.loop(0, ZS + LAG)
+    def _(turn):
+        @pl.when(turn < ZS)
+        def _():
+            @pl.when(turn > 0)
+            def _():
+                column_copy(turn).wait_recv()
+
+            spread(turn)
+
+        @pl.when(turn >= LAG)
+        def _():
+            ready = turn - LAG
+            own_copy(ready).wait()
+            all_of_plane(ready, plane_recv).wait()
+
+            @pl.loop(0, XS)
+            def _(part):
+                compute(slot(ready), part)
 
     def fold(unit):
         result = []
@@ -300,7 +318,6 @@
 
     for unit in range(16):
         partner_part[unit] = fold(unit)
-    swaps = []
     swap = pltpu.make_async_remote_copy(
         src_ref=partner_part,
         dst_ref=arrived_part,
@@ -317,13 +334,10 @@
         out_ref[0, :, unit * LANES : (unit + 1) * LANES] += arrived_part[unit]
 
     swap.wait_send()
-    for copy in sends:
-        copy.wait_send()
-    for hop in range(4):
-        for part in range(XS):
-            for way in (0, 1):
-                if hop < 3 or part == way:
-                    ring_copy(way, hop, part).wait_send()
+    for turn in range(ZS):
+        if turn > 0:
+            column_copy(turn).wait_send()
+        all_of_plane(turn, plane_send).wait()
 
 
 def body(sinogram, paganin_width, window_block):
@@ -341,21 +355,21 @@
             pltpu.VMEM((272, LANES), F32),
             pltpu.VMEM((272, LANES), F32),
             pltpu.VMEM((BLOCKS - 1, 8, LANES), F32),
-            pltpu.VMEM((TILES, KEEP, 8, LANES), BF16),
-            pltpu.VMEM((ZS, XS, TILES, KEEP, 8, LANES), BF16),
+            pltpu.VMEM((ZS, TILES, KEEP, 8, LANES), BF16),
+            pltpu.VMEM((ZS, XS * TILES, KEEP, 8, LANES), BF16),
             pltpu.VMEM((32, 64, LANES), F32),
             pltpu.VMEM((16, 32, LANES), F32),
             pltpu.VMEM((16, 32, LANES), F32),
-            pltpu.SemaphoreType.DMA((XS * TILES,)),
-            pltpu.SemaphoreType.DMA((XS * TILES,)),
-            pltpu.SemaphoreType.DMA((2, 4, XS)),
-            pltpu.SemaphoreType.DMA((2, 4, XS)),
-            pltpu.SemaphoreType.DMA,
+            pltpu.SemaphoreType.DMA((ZS,)),
+            pltpu.SemaphoreType.DMA((ZS,)),
+            pltpu.SemaphoreType.DMA((ZS,)),
+            pltpu.SemaphoreType.DMA((ZS,)),
+            pltpu.SemaphoreType.DMA((ZS,)),
             pltpu.SemaphoreType.DMA,
             pltpu.SemaphoreType.DMA,
         ],
         compiler_params=pltpu.CompilerParams(collective_id=0, has_side_effects=True),
-    )(sinogram, paganin_width, window_block, cosines, sines)
+    )(sinogram, paganin_width, window_block.T, cosines, sines)
 
 
 def solution(mesh):

time: 38.8 us -> 39 us (level)
  Pallas kernels: 34.9 us -> 36.5 us
  local copies, waits for them, and re-layouts: 3.06 us -> 1.67 us
    pallas_call x1, Pallas kernels: 34.9 us -> 36.5 us  [body(): pl.pallas_call(kernel, out_shape=jax.ShapeDtypeStruct((1, 32, ROWS_DEV *...]
    unnamed x2 -> x1, local copies, waits for them, and re-layouts: 3.06 us -> 1.67 us
where the time goes in v2:
time: 39 us; the launch traced here: 38.9 us
  Pallas kernels  36.5 us (94%)
  local copies, waits for them, and re-layouts  1.67 us (4%)
  between operations  0.66 us (2%)
    pallas_call x1, Pallas kernels, body(): pl.pallas_call(kernel, out_shape=jax.ShapeDtypeStruct((1, 32, ROWS_DEV *...  36.5 us
    unnamed x1, local copies, waits for them, and re-layouts  1.67 us

profile of v2, /device:TPU:1, one launch (start us, length us, event | category | flops | bytes accessed | tf_op | source)
XLA Modules:
  0.0 38.9 jit_solution(17339457080013597198)
XLA Ops:
  0.7 36.5 %shard_map.55 = f32[1,32,2048]{2,1,0:T(8,128)} custom-call(f32[2,4,4096]{2,1,0:T(4,128)} %sino_ref.1, f32[1]{0:T(128)S(6)} %copy.7.width_ref, s32[8,64]{1,0:T(8,128)} %bitcast.1, f32[64]{0:T(128)} %constant.4.clone.cos_ref, f32[64]{0:T(128)} %constant.5.clone.sin_ref), custom_call_target="tpu_custom_call" | custom-call | tf_op jit(solution)/shard_map/pallas_call | solution.py:349
  37.2 1.7 %copy.8 = f32[1,32,2048]{2,1,0:T(8,128)} copy(f32[1,32,2048]{2,1,0:T(8,128)} %shard_map.55) | data formatting | bytes 524288

commit v3 on v2

--- a/solution.py
+++ b/solution.py
@@ -23,7 +23,7 @@
 KEEP = 3
 BINS_SHIFT = 64
 CENTRE = 256 - BINS_SHIFT
-LAG = 3
+COLUMN = (1, -1, 2, -2)
 
 
 def ring_distance(step):
@@ -142,22 +142,22 @@
     x = (tile % 2) * 2 + chip // ZS
     y = tile // 2
 
-    def plane_peer(step):
+    def plane_peer(step, rise=0):
         other_x = (x + step[0]) % 4
         other_y = (y + step[1]) % 4
         other_tile = other_y * 2 + other_x // 2
-        return other_tile, (core, (other_x % 2) * ZS + z, other_tile)
-
-    def column_peer(shift):
-        return (core, chip - z + (z + shift) % ZS, tile)
+        return other_tile, (core, (other_x % 2) * ZS + (z + rise) % ZS, other_tile)
+
+    def column_peer(rise):
+        return (core, chip - z + (z + rise) % ZS, tile)
 
     partner = (1 - core, chip, tile)
 
     barrier = pltpu.get_barrier_semaphore()
     for step in PLANE_STEPS:
         pl.semaphore_signal(barrier, inc=1, device_id=plane_peer(step)[1], device_id_type=MESH)
-    for shift in range(1, ZS):
-        pl.semaphore_signal(barrier, inc=1, device_id=column_peer(shift), device_id_type=MESH)
+    for rise in COLUMN:
+        pl.semaphore_signal(barrier, inc=1, device_id=column_peer(rise), device_id_type=MESH)
     pl.semaphore_signal(barrier, inc=1, device_id=partner, device_id_type=MESH)
 
     filter_rows(sino_ref, width_ref, padded, smooth, filtered)
@@ -172,54 +172,84 @@
                 lower, filtered[first + block], filtered[second + block]
             ).astype(BF16)
 
+    pl.semaphore_wait(barrier, len(PLANE_STEPS) + len(COLUMN) + 1)
+
+    def column_copy(rise):
+        return pltpu.make_async_remote_copy(
+            src_ref=column.at[z],
+            dst_ref=column.at[z],
+            send_sem=column_send.at[rise % ZS],
+            recv_sem=column_recv.at[rise % ZS],
+            device_id=column_peer(rise),
+            device_id_type=MESH,
+        )
+
+    def slot(shift):
+        return (z + ZS - shift) % ZS
+
+    def own_copy(shift):
+        return pltpu.make_async_copy(
+            column.at[slot(shift), tile], held.at[slot(shift), spot], local_sem.at[shift]
+        )
+
+    def spread(shift, rise):
+        source = slot(shift)
+        arrival = (shift + rise) % ZS
+        steps = PLANE_STEPS
+        if rise:
+            steps = steps + [(0, 0)]
+        else:
+            own_copy(shift).start()
+        for step in steps:
+            other_tile, device = plane_peer(step, rise)
+            pltpu.make_async_remote_copy(
+                src_ref=column.at[source, other_tile],
+                dst_ref=held.at[source, spot],
+                send_sem=plane_send.at[arrival],
+                recv_sem=plane_recv.at[arrival],
+                device_id=device,
+                device_id_type=MESH,
+            ).start()
+
+    def all_of_plane(shift, sem, count):
+        some = held.at[slot(shift), pl.ds(0, count)]
+        return pltpu.make_async_copy(some, some, sem.at[shift])
+
+    def arrive(shift):
+        if shift in (3, 4, 5):
+            all_of_plane(shift, plane_recv, XS * TILES).wait()
+        else:
+            own_copy(shift).wait()
+            all_of_plane(shift, plane_recv, XS * TILES - 1).wait()
+
+    for rise in COLUMN:
+        column_copy(rise).start()
+    spread(0, 0)
+
     @pl.loop(0, 32)
     def _(unit):
         total[unit] = jnp.zeros((64, LANES), F32)
 
-    pl.semaphore_wait(barrier, len(PLANE_STEPS) + ZS)
-
-    def column_shift(turn):
-        far = (ZS + 1 - turn) // 2
-        return jnp.where(turn == 0, 0, jnp.where(turn % 2 == 0, far, ZS - far))
-
-    def column_copy(turn):
-        return pltpu.make_async_remote_copy(
-            src_ref=column.at[z],
-            dst_ref=column.at[z],
-            send_sem=column_send.at[turn],
-            recv_sem=column_recv.at[turn],
-            device_id=column_peer(column_shift(turn)),
-            device_id_type=MESH,
-        )
-
-    for turn in range(1, ZS):
-        column_copy(turn).start()
-
-    def slot(turn):
-        return (z + ZS - column_shift(turn)) % ZS
-
-    def own_copy(turn):
-        return pltpu.make_async_copy(
-            column.at[slot(turn), tile], held.at[slot(turn), spot], local_sem.at[turn]
-        )
-
-    def spread(turn):
-        source = slot(turn)
-        own_copy(turn).start()
-        for step in PLANE_STEPS:
-            other_tile, device = plane_peer(step)
-            pltpu.make_async_remote_copy(
-                src_ref=column.at[source, other_tile],
-                dst_ref=held.at[source, spot],
-                send_sem=plane_send.at[turn],
-                recv_sem=plane_recv.at[turn],
-                device_id=device,
-                device_id_type=MESH,
-            ).start()
-
-    def all_of_plane(turn, sem):
-        some = held.at[slot(turn), pl.ds(0, len(PLANE_STEPS))]
-        return pltpu.make_async_copy(some, some, sem.at[turn])
+    for rise in COLUMN[:2]:
+        column_copy(rise).wait_recv()
+        spread(rise % ZS, 0)
+    arrive(0)
+    column_copy(2).wait_recv()
+
+    @pl.when(core == 0)
+    def _():
+        spread(2, 2)
+
+    spread(2, 1)
+    column_copy(-2).wait_recv()
+
+    @pl.when(core == 1)
+    def _():
+        spread(ZS - 2, -2)
+
+    spread(ZS - 2, -1)
+    spread(2, 0)
+    spread(ZS - 2, 0)
 
     lane = iota((8, LANES), 1)
     lane_f = lane.astype(F32)
@@ -286,25 +316,13 @@
                         at = slice(pair * 16 + half_row * 8, pair * 16 + half_row * 8 + 8)
                         total[unit, at] += v[rows] + part_way * d[rows]
 
-    @pl.loop(0, ZS + LAG)
-    def _(turn):
-        @pl.when(turn < ZS)
-        def _():
-            @pl.when(turn > 0)
-            def _():
-                column_copy(turn).wait_recv()
-
-            spread(turn)
-
-        @pl.when(turn >= LAG)
-        def _():
-            ready = turn - LAG
-            own_copy(ready).wait()
-            all_of_plane(ready, plane_recv).wait()
-
-            @pl.loop(0, XS)
-            def _(part):
-                compute(slot(ready), part)
+    for shift in (0, 1, 7, 2, 6, 3, 5, 4):
+        if shift:
+            arrive(shift)
+
+        @pl.loop(0, XS)
+        def _(part):
+            compute(slot(shift), part)
 
     def fold(unit):
         result = []
@@ -334,10 +352,10 @@
         out_ref[0, :, unit * LANES : (unit + 1) * LANES] += arrived_part[unit]
 
     swap.wait_send()
-    for turn in range(ZS):
-        if turn > 0:
-            column_copy(turn).wait_send()
-        all_of_plane(turn, plane_send).wait()
+    for rise in COLUMN:
+        column_copy(rise).wait_send()
+    for shift in range(ZS):
+        all_of_plane(shift, plane_send, XS * TILES - (shift not in (3, 4, 5))).wait()
 
 
 def body(sinogram, paganin_width, window_block):

time: 39 us -> 34.1 us (0.87)
  Pallas kernels: 36.5 us -> 31.7 us
    pallas_call x1, Pallas kernels: 36.5 us -> 31.7 us  [body(): pl.pallas_call(kernel, out_shape=jax.ShapeDtypeStruct((1, 32, ROWS_DEV *...]
where the time goes in v3:
time: 34.1 us; the launch traced here: 34 us
  Pallas kernels  31.7 us (93%)
  local copies, waits for them, and re-layouts  1.67 us (5%)
  between operations  0.66 us (2%)
    pallas_call x1, Pallas kernels, body(): pl.pallas_call(kernel, out_shape=jax.ShapeDtypeStruct((1, 32, ROWS_DEV *...  31.7 us
    unnamed x1, local copies, waits for them, and re-layouts  1.67 us

profile of v3, /device:TPU:1, one launch (start us, length us, event | category | flops | bytes accessed | tf_op | source)
XLA Modules:
  0.0 34.0 jit_solution(16052392262714420816)
XLA Ops:
  0.7 31.7 %shard_map.55 = f32[1,32,2048]{2,1,0:T(8,128)} custom-call(f32[2,4,4096]{2,1,0:T(4,128)} %sino_ref.1, f32[1]{0:T(128)S(6)} %copy.7.width_ref, s32[8,64]{1,0:T(8,128)} %bitcast.1, f32[64]{0:T(128)} %constant.4.clone.cos_ref, f32[64]{0:T(128)} %constant.5.clone.sin_ref), custom_call_target="tpu_custom_call" | custom-call | tf_op jit(solution)/shard_map/pallas_call | solution.py:367
  32.3 1.7 %copy.8 = f32[1,32,2048]{2,1,0:T(8,128)} copy(f32[1,32,2048]{2,1,0:T(8,128)} %shard_map.55) | data formatting | bytes 524288

commit v4 on v3

--- a/solution.py
+++ b/solution.py
@@ -24,6 +24,7 @@
 BINS_SHIFT = 64
 CENTRE = 256 - BINS_SHIFT
 COLUMN = (1, -1, 2, -2)
+ORDER = (0, 1, 7, 4, 3, 5, 2, 6)
 
 
 def ring_distance(step):
@@ -118,6 +119,7 @@
     cos_ref,
     sin_ref,
     out_ref,
+    arrived_part,
     padded,
     smooth,
     filtered,
@@ -125,7 +127,9 @@
     held,
     total,
     partner_part,
-    arrived_part,
+    index_table,
+    start_table,
+    fraction_table,
     column_send,
     column_recv,
     plane_send,
@@ -226,64 +230,17 @@
         column_copy(rise).start()
     spread(0, 0)
 
-    @pl.loop(0, 32)
-    def _(unit):
-        total[unit] = jnp.zeros((64, LANES), F32)
-
-    for rise in COLUMN[:2]:
-        column_copy(rise).wait_recv()
-        spread(rise % ZS, 0)
-    arrive(0)
-    column_copy(2).wait_recv()
-
-    @pl.when(core == 0)
-    def _():
-        spread(2, 2)
-
-    spread(2, 1)
-    column_copy(-2).wait_recv()
-
-    @pl.when(core == 1)
-    def _():
-        spread(ZS - 2, -2)
-
-    spread(ZS - 2, -1)
-    spread(2, 0)
-    spread(ZS - 2, 0)
-
-    lane = iota((8, LANES), 1)
-    lane_f = lane.astype(F32)
+    lane_f = iota((8, LANES), 1).astype(F32)
     lane16 = iota((16, LANES), 1).astype(jnp.int16)
-    last_lane = lane == LANES - 1
+    last_lane = lane16 == jnp.int16(LANES - 1)
     own_row = ((core * XS * ZS + chip) * ROWS_DEV).astype(F32) - (TROWS - 1) / 2.0
     partner_row = (((1 - core) * XS * ZS + chip) * ROWS_DEV).astype(F32) - (TROWS - 1) / 2.0
 
-    def compute(source, part):
-        angle = (core * XS * ZS + part * ZS + source) * 2
-        spots = part * TILES
+    @pl.loop(0, XS * ZS)
+    def _(which):
+        angle = (core * XS * ZS + which) * 2
         cosine = jnp.where(lower, cos_ref[angle], cos_ref[angle + 1])
         sine = jnp.where(lower, sin_ref[angle], sin_ref[angle + 1])
-        values, slopes = [], []
-        for pair in range(TILES // 2):
-            value_row, slope_row = [], []
-            here = [
-                [held[source, spots + 2 * pair + half, block].astype(F32) for block in range(KEEP)]
-                for half in (0, 1)
-            ]
-            moved = [[pltpu.roll(v, LANES - 1, 1) for v in row] for row in here]
-            for block in range(KEEP):
-                diffs = []
-                for half in (0, 1):
-                    after = moved[half][min(block + 1, KEEP - 1)]
-                    diffs.append(
-                        jnp.where(last_lane, after, moved[half][block]) - here[half][block]
-                    )
-                value_row.append(
-                    jnp.concatenate([here[0][block], here[1][block]], axis=0).astype(BF16)
-                )
-                slope_row.append(jnp.concatenate(diffs, axis=0).astype(BF16))
-            values.append(value_row)
-            slopes.append(slope_row)
         spans, starts = [], []
         for half in (0, 1):
             left_end = half * LANES - (TCOLS - 1) / 2.0
@@ -297,32 +254,80 @@
                 unit = row * 2 + half
                 u = spans[half] + lift
                 k = u.astype(jnp.int32)
-                part_way = u - k.astype(F32)
+                fraction_table[which, unit] = u - k.astype(F32)
                 k = k & (LANES - 1)
-                index = jnp.concatenate([k, k], axis=0).astype(jnp.int16)
+                index_table[which, unit] = jnp.concatenate([k, k], axis=0).astype(jnp.int16)
                 begin = (starts[half] + lift).astype(jnp.int32)
-                begin = jnp.concatenate([begin, begin], axis=0).astype(jnp.int16)
-                past0 = begin > lane16
-                past1 = begin > lane16 + jnp.int16(LANES)
-                for pair in range(TILES // 2):
-                    v = values[pair]
-                    d = slopes[pair]
-                    v = jnp.where(past1, v[2], jnp.where(past0, v[1], v[0]))
-                    d = jnp.where(past1, d[2], jnp.where(past0, d[1], d[0]))
-                    v = lane_gather(v, index).astype(F32)
-                    d = lane_gather(d, index).astype(F32)
-                    for half_row in (0, 1):
-                        rows = slice(half_row * 8, half_row * 8 + 8)
-                        at = slice(pair * 16 + half_row * 8, pair * 16 + half_row * 8 + 8)
-                        total[unit, at] += v[rows] + part_way * d[rows]
-
-    for shift in (0, 1, 7, 2, 6, 3, 5, 4):
-        if shift:
-            arrive(shift)
-
-        @pl.loop(0, XS)
-        def _(part):
-            compute(slot(shift), part)
+                start_table[which, unit] = jnp.concatenate([begin, begin], axis=0).astype(
+                    jnp.int16
+                )
+
+    def sources(source, part):
+        values, slopes = [], []
+        for pair in range(TILES // 2):
+            first = part * TILES + 2 * pair
+            here = [
+                jnp.concatenate(
+                    [held[source, first, block], held[source, first + 1, block]], axis=0
+                )
+                for block in range(KEEP)
+            ]
+            moved = [pltpu.roll(v, LANES - 1, 1) for v in here]
+            values.append(here)
+            slopes.append(
+                [
+                    jnp.where(last_lane, moved[min(block + 1, KEEP - 1)], moved[block])
+                    - here[block]
+                    for block in range(KEEP)
+                ]
+            )
+        return values, slopes
+
+    def compute(source, part, units, fresh=False):
+        which = part * ZS + source
+        values, slopes = sources(source, part)
+        for unit in units:
+            index = index_table[which, unit]
+            begin = start_table[which, unit]
+            part_way = fraction_table[which, unit]
+            past0 = begin > lane16
+            past1 = begin > lane16 + jnp.int16(LANES)
+            for pair in range(TILES // 2):
+                v = values[pair]
+                d = slopes[pair]
+                v = jnp.where(past1, v[2], jnp.where(past0, v[1], v[0]))
+                d = jnp.where(past1, d[2], jnp.where(past0, d[1], d[0]))
+                v = lane_gather(v, index).astype(F32)
+                d = lane_gather(d, index).astype(F32)
+                for half_row in (0, 1):
+                    rows = slice(half_row * 8, half_row * 8 + 8)
+                    at = slice(pair * 16 + half_row * 8, pair * 16 + half_row * 8 + 8)
+                    term = v[rows] + part_way * d[rows]
+                    if fresh:
+                        total[unit, at] = term
+                    else:
+                        total[unit, at] += term
+
+    for rise in COLUMN[:2]:
+        column_copy(rise).wait_recv()
+        spread(rise % ZS, 0)
+    arrive(0)
+    column_copy(2).wait_recv()
+
+    @pl.when(core == 0)
+    def _():
+        spread(2, 2)
+
+    spread(2, 1)
+    column_copy(-2).wait_recv()
+
+    @pl.when(core == 1)
+    def _():
+        spread(ZS - 2, -2)
+
+    spread(ZS - 2, -1)
+    spread(2, 0)
+    spread(ZS - 2, 0)
 
     def fold(unit):
         result = []
@@ -334,8 +339,18 @@
             result.append(jnp.where(lower, pieces[0], pieces[1]))
         return jnp.concatenate(result, axis=0)
 
-    for unit in range(16):
-        partner_part[unit] = fold(unit)
+    theirs, ours = range(16), range(16, 32)
+    for shift in ORDER[:-1]:
+        if shift:
+            arrive(shift)
+        for part in range(XS):
+            compute(slot(shift), part, range(32), fresh=shift == 0 and part == 0)
+
+    arrive(ORDER[-1])
+    for part in range(XS):
+        compute(slot(ORDER[-1]), part, theirs)
+    for unit in theirs:
+        partner_part[0, :, unit * LANES : (unit + 1) * LANES] = fold(unit)
     swap = pltpu.make_async_remote_copy(
         src_ref=partner_part,
         dst_ref=arrived_part,
@@ -345,13 +360,11 @@
         device_id_type=MESH,
     )
     swap.start()
-    for unit in range(16):
-        out_ref[0, :, unit * LANES : (unit + 1) * LANES] = fold(unit + 16)
-    swap.wait_recv()
-    for unit in range(16):
-        out_ref[0, :, unit * LANES : (unit + 1) * LANES] += arrived_part[unit]
-
-    swap.wait_send()
+    for part in range(XS):
+        compute(slot(ORDER[-1]), part, ours)
+    for unit in ours:
+        out_ref[0, :, (unit - 16) * LANES : (unit - 15) * LANES] = fold(unit)
+    swap.wait()
     for rise in COLUMN:
         column_copy(rise).wait_send()
     for shift in range(ZS):
@@ -364,11 +377,12 @@
     sines = jnp.asarray(np.sin(angles).astype(np.float32))
     smem = pl.BlockSpec(memory_space=pltpu.SMEM)
     vmem = pl.BlockSpec(memory_space=pltpu.VMEM)
-    return pl.pallas_call(
+    part = jax.ShapeDtypeStruct((1, 32, ROWS_DEV * TCOLS), F32)
+    own, arrived = pl.pallas_call(
         kernel,
-        out_shape=jax.ShapeDtypeStruct((1, 32, ROWS_DEV * TCOLS), F32),
+        out_shape=(part, part),
         in_specs=[vmem, smem, smem, smem, smem],
-        out_specs=vmem,
+        out_specs=(vmem, vmem),
         scratch_shapes=[
             pltpu.VMEM((272, LANES), F32),
             pltpu.VMEM((272, LANES), F32),
@@ -376,8 +390,10 @@
             pltpu.VMEM((ZS, TILES, KEEP, 8, LANES), BF16),
             pltpu.VMEM((ZS, XS * TILES, KEEP, 8, LANES), BF16),
             pltpu.VMEM((32, 64, LANES), F32),
-            pltpu.VMEM((16, 32, LANES), F32),
-            pltpu.VMEM((16, 32, LANES), F32),
+            pltpu.VMEM((1, 32, ROWS_DEV * TCOLS), F32),
+            pltpu.VMEM((XS * ZS, 32, 16, LANES), jnp.int16),
+            pltpu.VMEM((XS * ZS, 32, 16, LANES), jnp.int16),
+            pltpu.VMEM((XS * ZS, 32, 8, LANES), F32),
             pltpu.SemaphoreType.DMA((ZS,)),
             pltpu.SemaphoreType.DMA((ZS,)),
             pltpu.SemaphoreType.DMA((ZS,)),
@@ -386,8 +402,11 @@
             pltpu.SemaphoreType.DMA,
             pltpu.SemaphoreType.DMA,
         ],
-        compiler_params=pltpu.CompilerParams(collective_id=0, has_side_effects=True),
+        compiler_params=pltpu.CompilerParams(
+            collective_id=0, has_side_effects=True, vmem_limit_bytes=32 << 20
+        ),
     )(sinogram, paganin_width, window_block.T, cosines, sines)
+    return own + arrived
 
 
 def solution(mesh):

time: 34.1 us -> 34 us (level)
  Pallas kernels: 31.7 us -> 30.2 us
  other arithmetic: 0 us -> 0.73 us
  local copies, waits for them, and re-layouts: 1.67 us -> 2.25 us
    pallas_call x1, Pallas kernels: 31.7 us -> 30.2 us  [body(): pl.pallas_call(kernel, out_shape=(part, part), in_specs=[vmem, smem, smem...]
    add x0 -> x1, other arithmetic: none -> 0.73 us  [body(): return own + arrived]
    unnamed x1 -> x8, local copies, waits for them, and re-layouts: 1.67 us -> 2.25 us
where the time goes in v4:
time: 34 us; the launch traced here: 33.8 us
  Pallas kernels  30.2 us (89%)
  local copies, waits for them, and re-layouts  2.25 us (7%)
  other arithmetic  0.73 us (2%)
  between operations  0.68 us (2%)
    pallas_call x1, Pallas kernels, body(): pl.pallas_call(kernel, out_shape=(part, part), in_specs=[vmem, smem, smem...  30.2 us
    unnamed x8, local copies, waits for them, and re-layouts  2.25 us
    add x1, other arithmetic, body(): return own + arrived  0.73 us

profile of v4, /device:TPU:1, one launch (start us, length us, event | category | flops | bytes accessed | tf_op | source)
XLA Modules:
  0.0 33.8 jit_solution(14529899433081602827)
XLA Ops:
  0.7 0.0 copy-start.2
  0.7 0.0 copy-start.3
  0.7 0.6 %copy-done.2 = f32[64]{0:T(128)S(1)} copy-done((f32[64]{0:T(128)S(1)}, f32[64]{0:T(128)}, u32[]{:S(2)}) %copy-start.2) | copy-done | bytes 280
  1.3 0.0 copy-done.3
  1.3 0.0 copy-start
  1.3 0.9 %copy-done = f32[2,4,4096]{2,1,0:T(4,128)S(1)} copy-done((f32[2,4,4096]{2,1,0:T(4,128)S(1)}, f32[2,4,4096]{2,1,0:T(4,128)}, u32[]{:S(2)}) %copy-start) | copy-done | bytes 131096
  2.2 0.0 copy-start.1
  2.2 0.7 %copy-done.1 = s32[64,8]{0,1:T(8,128)S(1)} copy-done((s32[64,8]{0,1:T(8,128)S(1)}, s32[64,8]{0,1:T(8,128)}, u32[]{:S(2)}) %copy-start.1) | copy-done | bytes 2072
  2.9 30.2 %shard_map.55 = (f32[1,32,2048]{2,1,0:T(8,128)S(1)}, f32[1,32,2048]{2,1,0:T(8,128)S(1)}) custom-call(f32[2,4,4096]{2,1,0:T(4,128)S(1)} %copy-done, f32[1]{0:T(128)S(6)} %copy.6.width_ref, s32[8,64]{1,0:T(8,128)S(1)} %bitcast.1, f32[64]{0:T(128)S(1)} %copy-done.3, f32[64]{0:T(128)S(1)} %copy-done.2), custom_call_target="tpu_custom_call" | custom-call | tf_op jit(solution)/shard_map/pallas_call | solution.py:381
  33.1 0.7 %add.3 = f32[1,32,2048]{2,1,0:T(8,128)} add(f32[1,32,2048]{2,1,0:T(8,128)S(1)} %get-tuple-element.7, f32[1,32,2048]{2,1,0:T(8,128)S(1)} %get-tuple-element.8) | non-fusion elementwise | flops 65536 | bytes 786432 | tf_op jit(solution)/shard_map/add | solution.py:409
Async XLA Ops:
  0.7 0.7 %copy-start.2 = (f32[64]{0:T(128)S(1)}, f32[64]{0:T(128)}, u32[]{:S(2)}) copy-start(f32[64]{0:T(128)} %constant.5.clone.sin_ref) | copy-start | bytes 772
  0.7 0.7 %copy-start.3 = (f32[64]{0:T(128)S(1)}, f32[64]{0:T(128)}, u32[]{:S(2)}) copy-start(f32[64]{0:T(128)} %constant.4.clone.cos_ref) | copy-start | bytes 772
  1.3 0.9 %copy-start = (f32[2,4,4096]{2,1,0:T(4,128)S(1)}, f32[2,4,4096]{2,1,0:T(4,128)}, u32[]{:S(2)}) copy-start(f32[2,4,4096]{2,1,0:T(4,128)} %sino_ref.1) | copy-start | bytes 393220
  2.2 0.7 %copy-start.1 = (s32[64,8]{0,1:T(8,128)S(1)}, s32[64,8]{0,1:T(8,128)}, u32[]{:S(2)}) copy-start(s32[64,8]{0,1:T(8,128)} %param.7) | copy-start | bytes 6148

commit v5 on v4

--- a/solution.py
+++ b/solution.py
@@ -3,7 +3,6 @@
 
 import jax
 import jax.numpy as jnp
-import numpy as np
 from jax import lax
 from jax.experimental import pallas as pl
 from jax.experimental.pallas import tpu as pltpu
@@ -94,32 +93,34 @@
     return jnp.where(offset == 0, 0.25, odd)
 
 
-def filter_rows(sino_ref, width_ref, padded, smooth, filtered):
+def filter_rows(sino_copy, sino_ref, width_ref, padded, smooth, filtered):
+    smoothing = smoothing_band(jnp.full((1, 1), width_ref[0], F32))
+    ramp = ramp_band()
     zero = jnp.zeros((8, LANES), F32)
     padded[0:8] = zero
     padded[264:272] = zero
     smooth[0:8] = zero
     smooth[264:272] = zero
+    sino_copy.wait()
     for block in range(BLOCKS):
         columns = slice(block * LANES, (block + 1) * LANES)
         padded[(block + 1) * 8 : (block + 2) * 8] = jnp.concatenate(
             [sino_ref[0, :, columns], sino_ref[1, :, columns]], axis=0
         )
     left = jnp.concatenate([padded[8 * k : 8 * k + 256] for k in range(3)], axis=1)
-    width = jnp.full((1, 1), width_ref[0], F32)
-    smooth[8:264] = dot3(left, smoothing_band(width))
+    smooth[8:264] = dot3(left, smoothing)
     left = jnp.concatenate([smooth[8 * k : 8 * k + 248] for k in range(4)], axis=1)
-    filtered[...] = dot3(left, ramp_band()).reshape(BLOCKS - 1, 8, LANES)
+    filtered[...] = dot3(left, ramp).reshape(BLOCKS - 1, 8, LANES)
 
 
 def kernel(
-    sino_ref,
+    sino_hbm,
     width_ref,
-    window_ref,
-    cos_ref,
-    sin_ref,
+    window_hbm,
     out_ref,
     arrived_part,
+    sino_ref,
+    window_ref,
     padded,
     smooth,
     filtered,
@@ -130,6 +131,7 @@
     index_table,
     start_table,
     fraction_table,
+    input_sem,
     column_send,
     column_recv,
     plane_send,
@@ -138,6 +140,10 @@
     part_send,
     part_recv,
 ):
+    sino_copy = pltpu.make_async_copy(sino_hbm, sino_ref, input_sem.at[0])
+    window_copy = pltpu.make_async_copy(window_hbm, window_ref, input_sem.at[1])
+    sino_copy.start()
+    window_copy.start()
     core = lax.axis_index("segment")
     chip = lax.axis_index("angle")
     tile = lax.axis_index("tile")
@@ -164,7 +170,8 @@
         pl.semaphore_signal(barrier, inc=1, device_id=column_peer(rise), device_id_type=MESH)
     pl.semaphore_signal(barrier, inc=1, device_id=partner, device_id_type=MESH)
 
-    filter_rows(sino_ref, width_ref, padded, smooth, filtered)
+    filter_rows(sino_copy, sino_ref, width_ref, padded, smooth, filtered)
+    window_copy.wait()
 
     lower = iota((8, LANES), 0) < 4
     first_angle = (core * XS * ZS + chip) * 2
@@ -239,8 +246,8 @@
     @pl.loop(0, XS * ZS)
     def _(which):
         angle = (core * XS * ZS + which) * 2
-        cosine = jnp.where(lower, cos_ref[angle], cos_ref[angle + 1])
-        sine = jnp.where(lower, sin_ref[angle], sin_ref[angle + 1])
+        theta = jnp.where(lower, angle, angle + 1).astype(F32) * (math.pi / ANGLES)
+        cosine, sine = jnp.cos(theta), jnp.sin(theta)
         spans, starts = [], []
         for half in (0, 1):
             left_end = half * LANES - (TCOLS - 1) / 2.0
@@ -255,21 +262,22 @@
                 u = spans[half] + lift
                 k = u.astype(jnp.int32)
                 fraction_table[which, unit] = u - k.astype(F32)
-                k = k & (LANES - 1)
-                index_table[which, unit] = jnp.concatenate([k, k], axis=0).astype(jnp.int16)
-                begin = (starts[half] + lift).astype(jnp.int32)
-                start_table[which, unit] = jnp.concatenate([begin, begin], axis=0).astype(
-                    jnp.int16
-                )
-
-    def sources(source, part):
+                index_table[which, unit] = k & (LANES - 1)
+                start_table[which, unit] = (starts[half] + lift).astype(jnp.int32)
+
+    def compute(source, part, units):
+        which = part * ZS + source
         values, slopes = [], []
         for pair in range(TILES // 2):
             first = part * TILES + 2 * pair
             here = [
                 jnp.concatenate(
-                    [held[source, first, block], held[source, first + 1, block]], axis=0
-                )
+                    [
+                        held[source, first, block].astype(F32),
+                        held[source, first + 1, block].astype(F32),
+                    ],
+                    axis=0,
+                ).astype(BF16)
                 for block in range(KEEP)
             ]
             moved = [pltpu.roll(v, LANES - 1, 1) for v in here]
@@ -281,14 +289,11 @@
                     for block in range(KEEP)
                 ]
             )
-        return values, slopes
-
-    def compute(source, part, units, fresh=False):
-        which = part * ZS + source
-        values, slopes = sources(source, part)
         for unit in units:
             index = index_table[which, unit]
+            index = jnp.concatenate([index, index], axis=0).astype(jnp.int16)
             begin = start_table[which, unit]
+            begin = jnp.concatenate([begin, begin], axis=0).astype(jnp.int16)
             part_way = fraction_table[which, unit]
             past0 = begin > lane16
             past1 = begin > lane16 + jnp.int16(LANES)
@@ -303,10 +308,7 @@
                     rows = slice(half_row * 8, half_row * 8 + 8)
                     at = slice(pair * 16 + half_row * 8, pair * 16 + half_row * 8 + 8)
                     term = v[rows] + part_way * d[rows]
-                    if fresh:
-                        total[unit, at] = term
-                    else:
-                        total[unit, at] += term
+                    total[unit, at] += term
 
     for rise in COLUMN[:2]:
         column_copy(rise).wait_recv()
@@ -339,16 +341,22 @@
             result.append(jnp.where(lower, pieces[0], pieces[1]))
         return jnp.concatenate(result, axis=0)
 
+    def run(source, units):
+        for part in range(XS):
+            compute(source, part, units)
+
+    @pl.loop(0, 32)
+    def _(unit):
+        total[unit] = jnp.zeros((64, LANES), F32)
+
     theirs, ours = range(16), range(16, 32)
     for shift in ORDER[:-1]:
         if shift:
             arrive(shift)
-        for part in range(XS):
-            compute(slot(shift), part, range(32), fresh=shift == 0 and part == 0)
+        run(slot(shift), range(32))
 
     arrive(ORDER[-1])
-    for part in range(XS):
-        compute(slot(ORDER[-1]), part, theirs)
+    run(slot(ORDER[-1]), theirs)
     for unit in theirs:
         partner_part[0, :, unit * LANES : (unit + 1) * LANES] = fold(unit)
     swap = pltpu.make_async_remote_copy(
@@ -360,8 +368,7 @@
         device_id_type=MESH,
     )
     swap.start()
-    for part in range(XS):
-        compute(slot(ORDER[-1]), part, ours)
+    run(slot(ORDER[-1]), ours)
     for unit in ours:
         out_ref[0, :, (unit - 16) * LANES : (unit - 15) * LANES] = fold(unit)
     swap.wait()
@@ -372,18 +379,18 @@
 
 
 def body(sinogram, paganin_width, window_block):
-    angles = np.pi * np.arange(ANGLES) / ANGLES
-    cosines = jnp.asarray(np.cos(angles).astype(np.float32))
-    sines = jnp.asarray(np.sin(angles).astype(np.float32))
     smem = pl.BlockSpec(memory_space=pltpu.SMEM)
+    hbm = pl.BlockSpec(memory_space=pltpu.HBM)
     vmem = pl.BlockSpec(memory_space=pltpu.VMEM)
     part = jax.ShapeDtypeStruct((1, 32, ROWS_DEV * TCOLS), F32)
     own, arrived = pl.pallas_call(
         kernel,
         out_shape=(part, part),
-        in_specs=[vmem, smem, smem, smem, smem],
+        in_specs=[hbm, smem, hbm],
         out_specs=(vmem, vmem),
         scratch_shapes=[
+            pltpu.VMEM((2, 4, BLOCKS * LANES), F32),
+            pltpu.SMEM((TILES, ANGLES), jnp.int32),
             pltpu.VMEM((272, LANES), F32),
             pltpu.VMEM((272, LANES), F32),
             pltpu.VMEM((BLOCKS - 1, 8, LANES), F32),
@@ -391,9 +398,10 @@
             pltpu.VMEM((ZS, XS * TILES, KEEP, 8, LANES), BF16),
             pltpu.VMEM((32, 64, LANES), F32),
             pltpu.VMEM((1, 32, ROWS_DEV * TCOLS), F32),
-            pltpu.VMEM((XS * ZS, 32, 16, LANES), jnp.int16),
-            pltpu.VMEM((XS * ZS, 32, 16, LANES), jnp.int16),
+            pltpu.VMEM((XS * ZS, 32, 8, LANES), jnp.int32),
+            pltpu.VMEM((XS * ZS, 32, 8, LANES), jnp.int32),
             pltpu.VMEM((XS * ZS, 32, 8, LANES), F32),
+            pltpu.SemaphoreType.DMA((2,)),
             pltpu.SemaphoreType.DMA((ZS,)),
             pltpu.SemaphoreType.DMA((ZS,)),
             pltpu.SemaphoreType.DMA((ZS,)),
@@ -405,7 +413,7 @@
         compiler_params=pltpu.CompilerParams(
             collective_id=0, has_side_effects=True, vmem_limit_bytes=32 << 20
         ),
-    )(sinogram, paganin_width, window_block.T, cosines, sines)
+    )(sinogram, paganin_width, window_block.T)
     return own + arrived
 
 

time: 34 us -> 32.4 us (0.953)
  Pallas kernels: 30.2 us -> 29.2 us
  local copies, waits for them, and re-layouts: 2.25 us -> 1.58 us
    pallas_call x1, Pallas kernels: 30.2 us -> 29.2 us  [body(): pl.pallas_call(kernel, out_shape=(part, part), in_specs=[hbm, smem, hbm],...]
    unnamed x8 -> x4, local copies, waits for them, and re-layouts: 2.25 us -> 1.58 us
where the time goes in v5:
time: 32.4 us; the launch traced here: 32.2 us
  Pallas kernels  29.2 us (90%)
  local copies, waits for them, and re-layouts  1.58 us (5%)
  other arithmetic  0.73 us (2%)
  between operations  0.67 us (2%)
    pallas_call x1, Pallas kernels, body(): pl.pallas_call(kernel, out_shape=(part, part), in_specs=[hbm, smem, hbm],...  29.2 us
    unnamed x4, local copies, waits for them, and re-layouts  1.58 us
    add x1, other arithmetic, body(): return own + arrived  0.73 us

profile of v5, /device:TPU:1, one launch (start us, length us, event | category | flops | bytes accessed | tf_op | source)
XLA Modules:
  0.0 32.2 jit_solution(11570270185820228565)
XLA Ops:
  0.7 0.0 copy-start
  0.7 0.9 %copy-done = f32[2,4,4096]{2,1,0:T(4,128)S(1)} copy-done((f32[2,4,4096]{2,1,0:T(4,128)S(1)}, f32[2,4,4096]{2,1,0:T(4,128)}, u32[]{:S(2)}) %copy-start) | copy-done | bytes 131096
  1.6 0.0 copy-start.1
  1.6 0.7 %copy-done.1 = s32[64,8]{0,1:T(8,128)S(1)} copy-done((s32[64,8]{0,1:T(8,128)S(1)}, s32[64,8]{0,1:T(8,128)}, u32[]{:S(2)}) %copy-start.1) | copy-done | bytes 2072
  2.2 29.2 %shard_map.37 = (f32[1,32,2048]{2,1,0:T(8,128)S(1)}, f32[1,32,2048]{2,1,0:T(8,128)S(1)}) custom-call(f32[2,4,4096]{2,1,0:T(4,128)S(1)} %copy-done, f32[1]{0:T(128)S(6)} %copy.4.width_ref, s32[8,64]{1,0:T(8,128)S(1)} %bitcast.1), custom_call_target="tpu_custom_call" | custom-call | tf_op jit(solution)/shard_map/pallas_call | solution.py:386
  31.5 0.7 %add.3 = f32[1,32,2048]{2,1,0:T(8,128)} add(f32[1,32,2048]{2,1,0:T(8,128)S(1)} %get-tuple-element.7, f32[1,32,2048]{2,1,0:T(8,128)S(1)} %get-tuple-element.8) | non-fusion elementwise | flops 65536 | bytes 786432 | tf_op jit(solution)/shard_map/add | solution.py:417
Async XLA Ops:
  0.7 0.9 %copy-start = (f32[2,4,4096]{2,1,0:T(4,128)S(1)}, f32[2,4,4096]{2,1,0:T(4,128)}, u32[]{:S(2)}) copy-start(f32[2,4,4096]{2,1,0:T(4,128)} %sino_hbm.1) | copy-start | bytes 393220
  1.6 0.7 %copy-start.1 = (s32[64,8]{0,1:T(8,128)S(1)}, s32[64,8]{0,1:T(8,128)}, u32[]{:S(2)}) copy-start(s32[64,8]{0,1:T(8,128)} %param.5) | copy-start | bytes 6148

commit v6 on v5

--- a/solution.py
+++ b/solution.py
@@ -413,7 +413,11 @@
         compiler_params=pltpu.CompilerParams(
             collective_id=0, has_side_effects=True, vmem_limit_bytes=32 << 20
         ),
-    )(sinogram, paganin_width, window_block.T)
+    )(
+        pltpu.with_memory_space_constraint(sinogram, pltpu.HBM),
+        paganin_width,
+        pltpu.with_memory_space_constraint(window_block.T, pltpu.HBM),
+    )
     return own + arrived
 
 

time: 32.4 us -> 30.7 us (0.948)
  local copies, waits for them, and re-layouts: 1.58 us -> 0 us
    unnamed x4 -> x0, local copies, waits for them, and re-layouts: 1.58 us -> none
where the time goes in v6:
time: 30.7 us; the launch traced here: 30.6 us
  Pallas kernels  29.2 us (95%)
  other arithmetic  0.73 us (2%)
  between operations  0.66 us (2%)
    pallas_call x1, Pallas kernels, body(): pl.pallas_call(kernel, out_shape=(part, part), in_specs=[hbm, smem, hbm],...  29.2 us
    add x1, other arithmetic, body(): return own + arrived  0.73 us

profile of v6, /device:TPU:1, one launch (start us, length us, event | category | flops | bytes accessed | tf_op | source)
XLA Modules:
  0.0 30.6 jit_solution(6292950985773658747)
XLA Ops:
  0.7 29.2 %shard_map.37 = (f32[1,32,2048]{2,1,0:T(8,128)S(1)}, f32[1,32,2048]{2,1,0:T(8,128)S(1)}) custom-call(f32[2,4,4096]{2,1,0:T(4,128)} %sino_hbm.1, f32[1]{0:T(128)S(6)} %copy.4.width_ref, s32[8,64]{1,0:T(8,128)} %bitcast.1), custom_call_target="tpu_custom_call" | custom-call | tf_op jit(solution)/shard_map/pallas_call | solution.py:386
  29.9 0.7 %add.3 = f32[1,32,2048]{2,1,0:T(8,128)} add(f32[1,32,2048]{2,1,0:T(8,128)S(1)} %get-tuple-element.7, f32[1,32,2048]{2,1,0:T(8,128)S(1)} %get-tuple-element.8) | non-fusion elementwise | flops 65536 | bytes 786432 | tf_op jit(solution)/shard_map/add | solution.py:421

commit v7 on v6

--- a/solution.py
+++ b/solution.py
@@ -23,7 +23,8 @@
 BINS_SHIFT = 64
 CENTRE = 256 - BINS_SHIFT
 COLUMN = (1, -1, 2, -2)
-ORDER = (0, 1, 7, 4, 3, 5, 2, 6)
+LATE = 3
+ORDER = (1, 7, 3, 5, 2, 6, 4)
 
 
 def ring_distance(step):
@@ -313,24 +314,6 @@
     for rise in COLUMN[:2]:
         column_copy(rise).wait_recv()
         spread(rise % ZS, 0)
-    arrive(0)
-    column_copy(2).wait_recv()
-
-    @pl.when(core == 0)
-    def _():
-        spread(2, 2)
-
-    spread(2, 1)
-    column_copy(-2).wait_recv()
-
-    @pl.when(core == 1)
-    def _():
-        spread(ZS - 2, -2)
-
-    spread(ZS - 2, -1)
-    spread(2, 0)
-    spread(ZS - 2, 0)
-
     def fold(unit):
         result = []
         for group in range(4):
@@ -349,14 +332,32 @@
     def _(unit):
         total[unit] = jnp.zeros((64, LANES), F32)
 
+    arrive(0)
+    spread(1, 2)
+    spread(ZS - 1, -2)
+    run(slot(0), range(32))
+
+    column_copy(2).wait_recv()
+    column_copy(-2).wait_recv()
+    spread(2, 0)
+    spread(ZS - 2, 0)
+
+    @pl.when(core == 0)
+    def _():
+        spread(2, 2)
+
+    @pl.when(core == 1)
+    def _():
+        spread(ZS - 2, -2)
+
     theirs, ours = range(16), range(16, 32)
-    for shift in ORDER[:-1]:
-        if shift:
-            arrive(shift)
+    for shift in ORDER[:-LATE]:
+        arrive(shift)
         run(slot(shift), range(32))
 
-    arrive(ORDER[-1])
-    run(slot(ORDER[-1]), theirs)
+    for shift in ORDER[-LATE:]:
+        arrive(shift)
+        run(slot(shift), theirs)
     for unit in theirs:
         partner_part[0, :, unit * LANES : (unit + 1) * LANES] = fold(unit)
     swap = pltpu.make_async_remote_copy(
@@ -368,7 +369,8 @@
         device_id_type=MESH,
     )
     swap.start()
-    run(slot(ORDER[-1]), ours)
+    for shift in ORDER[-LATE:]:
+        run(slot(shift), ours)
     for unit in ours:
         out_ref[0, :, (unit - 16) * LANES : (unit - 15) * LANES] = fold(unit)
     swap.wait()

time: 30.7 us -> 29.8 us (0.971)
  Pallas kernels: 29.2 us -> 28.3 us
    pallas_call x1, Pallas kernels: 29.2 us -> 28.3 us  [body(): pl.pallas_call(kernel, out_shape=(part, part), in_specs=[hbm, smem, hbm],...]
where the time goes in v7:
time: 29.8 us; the launch traced here: 29.7 us
  Pallas kernels  28.3 us (95%)
  other arithmetic  0.73 us (2%)
  between operations  0.66 us (2%)
    pallas_call x1, Pallas kernels, body(): pl.pallas_call(kernel, out_shape=(part, part), in_specs=[hbm, smem, hbm],...  28.3 us
    add x1, other arithmetic, body(): return own + arrived  0.73 us

profile of v7, /device:TPU:1, one launch (start us, length us, event | category | flops | bytes accessed | tf_op | source)
XLA Modules:
  0.0 29.7 jit_solution(3809364140717054856)
XLA Ops:
  0.7 28.3 %shard_map.37 = (f32[1,32,2048]{2,1,0:T(8,128)S(1)}, f32[1,32,2048]{2,1,0:T(8,128)S(1)}) custom-call(f32[2,4,4096]{2,1,0:T(4,128)} %sino_hbm.1, f32[1]{0:T(128)S(6)} %copy.4.width_ref, s32[8,64]{1,0:T(8,128)} %bitcast.1), custom_call_target="tpu_custom_call" | custom-call | tf_op jit(solution)/shard_map/pallas_call | solution.py:388
  28.9 0.7 %add.3 = f32[1,32,2048]{2,1,0:T(8,128)} add(f32[1,32,2048]{2,1,0:T(8,128)S(1)} %get-tuple-element.7, f32[1,32,2048]{2,1,0:T(8,128)S(1)} %get-tuple-element.8) | non-fusion elementwise | flops 65536 | bytes 786432 | tf_op jit(solution)/shard_map/add | solution.py:423

commit v8 on v7

--- a/solution.py
+++ b/solution.py
@@ -23,7 +23,7 @@
 BINS_SHIFT = 64
 CENTRE = 256 - BINS_SHIFT
 COLUMN = (1, -1, 2, -2)
-LATE = 3
+LATE = 5
 ORDER = (1, 7, 3, 5, 2, 6, 4)
 
 

time: 29.8 us -> 29 us (0.973)
  Pallas kernels: 28.3 us -> 27.5 us
    pallas_call x1, Pallas kernels: 28.3 us -> 27.5 us  [body(): pl.pallas_call(kernel, out_shape=(part, part), in_specs=[hbm, smem, hbm],...]
where the time goes in v8:
time: 29 us; the launch traced here: 28.9 us
  Pallas kernels  27.5 us (95%)
  other arithmetic  0.73 us (3%)
  between operations  0.66 us (2%)
    pallas_call x1, Pallas kernels, body(): pl.pallas_call(kernel, out_shape=(part, part), in_specs=[hbm, smem, hbm],...  27.5 us
    add x1, other arithmetic, body(): return own + arrived  0.73 us

profile of v8, /device:TPU:1, one launch (start us, length us, event | category | flops | bytes accessed | tf_op | source)
XLA Modules:
  0.0 28.9 jit_solution(13614002677390181666)
XLA Ops:
  0.7 27.5 %shard_map.37 = (f32[1,32,2048]{2,1,0:T(8,128)S(1)}, f32[1,32,2048]{2,1,0:T(8,128)S(1)}) custom-call(f32[2,4,4096]{2,1,0:T(4,128)} %sino_hbm.1, f32[1]{0:T(128)S(6)} %copy.4.width_ref, s32[8,64]{1,0:T(8,128)} %bitcast.1), custom_call_target="tpu_custom_call" | custom-call | tf_op jit(solution)/shard_map/pallas_call | solution.py:388
  28.2 0.7 %add.3 = f32[1,32,2048]{2,1,0:T(8,128)} add(f32[1,32,2048]{2,1,0:T(8,128)S(1)} %get-tuple-element.7, f32[1,32,2048]{2,1,0:T(8,128)S(1)} %get-tuple-element.8) | non-fusion elementwise | flops 65536 | bytes 786432 | tf_op jit(solution)/shard_map/add | solution.py:423
